TPU v7x, 512 devices: a whole 4x4x16 slice. The times are simulated.
512 devices in a mesh: sec: 64 (over x_hi, z, core), chol: 8 (over y, x_lo).
Axes of the slice: x: 4 (x_hi: 2, x_lo: 2; x = x_hi * 2 + x_lo), y: 4, z: 16, core: 2. Of those that a mesh axis runs over, the one named last changes fastest.
Arguments:
- amplitudes: bfloat16 [64, 16, 1024], P('sec'), may hold values from -3 to 3
- driver: bfloat16 [64, 16, 1024], P('sec'), may hold values from -24 to 24
- x_tiles: bfloat16 [64, 3, 3072, 1024], P('sec', None, 'chol'), may hold values from -0.15625 to 0.15625
- y_tiles: bfloat16 [64, 3, 3072, 1024], P('sec', None, 'chol'), may hold values from -0.15625 to 0.15625
- sources: int32 [64, 3], P('sec'), may hold values from 0 to 63
- live: int32 [64, 3], P('sec'), may hold values from 0 to 1, as said below
- block_tiles: int32 [64, 2], P('sec'), may hold values from 0 to 31
- pairs: int32 [16, 2], replicated, may hold values from 0 to 127
- e_virt: float32 [1024], replicated, may hold values from 0.5 to 3
- e_occ: float32 [128], replicated, may hold values from -2 to -0.3
Outputs:
- updated: bfloat16 [64, 16, 1024], P('sec')
Inputs may be any that keep to these rules, and one draw needn't show every extreme that they name: In every tile pair slot 0 is live and live slots come first; some tile pair has all 3 slots live.
All inputs are finite; a program needn't handle non-finite values.
Results may differ from a plain program's by a relative error of at most 0.003.
Values may be sent and summed in bfloat16 or wider, within the bound.
A program may use at most 64 MiB of HBM per device.

v0:
```python
import jax
import jax.numpy as jnp
from jax import lax
from jax.sharding import PartitionSpec as P

TS = 32
ITERS = 2


def integral(left_tile, right_tile):
    product = lax.dot_general(
        left_tile, right_tile, (((0,), (0,)), ((), ())), preferred_element_type=jnp.float32
    )
    product = product.reshape(TS, TS, TS, TS).transpose(1, 3, 0, 2)
    return product.reshape(TS * TS, TS * TS).astype(jnp.bfloat16)


def ladder(every, cached, source_ids, live_f):
    total = jnp.zeros((every.shape[1], every.shape[2]), jnp.float32)
    for slot_idx in range(len(cached)):
        picked = lax.dynamic_index_in_dim(every, source_ids[slot_idx], 0, keepdims=False)
        total = total + live_f[slot_idx] * jnp.dot(
            picked, cached[slot_idx], preferred_element_type=jnp.float32
        )
    return total


def shards(amplitudes, driver, x_tiles, y_tiles, sources, live, block_tiles, pairs, e_virt, e_occ):
    source_ids = sources[0]
    live_f = live[0].astype(jnp.float32)
    cached = []
    for slot_idx in range(x_tiles.shape[1]):
        left_tile = x_tiles[0, slot_idx]
        right_tile = y_tiles[0, slot_idx]
        built = integral(left_tile, right_tile)
        cached.append(built)
    tile_energy = e_virt.reshape(-1, TS)
    energy_a = lax.dynamic_index_in_dim(tile_energy, block_tiles[0, 0], 0, keepdims=False)
    energy_b = lax.dynamic_index_in_dim(tile_energy, block_tiles[0, 1], 0, keepdims=False)
    energy_ij = e_occ[pairs[:, 0]] + e_occ[pairs[:, 1]]
    denominator = (
        energy_a[None, :, None] + energy_b[None, None, :] - energy_ij[:, None, None]
    ).reshape(pairs.shape[0], TS * TS)
    driven = driver[0].astype(jnp.float32)
    every = lax.all_gather(amplitudes, "sec", axis=0, tiled=True)
    current = amplitudes
    for sweep in range(ITERS):
        final_sweep = sweep + 1 == ITERS
        local_sum = ladder(every, cached, source_ids, live_f)
        summed = lax.psum(local_sum, "chol")
        current = (-(driven + summed) / denominator).astype(jnp.bfloat16)[None]
        if not final_sweep:
            every = lax.all_gather(current, "sec", axis=0, tiled=True)
    return current


def solution(mesh):
    placed = (
        P("sec", None, None),
        P("sec", None, None),
        P("sec", None, "chol", None),
        P("sec", None, "chol", None),
        P("sec", None),
        P("sec", None),
        P("sec", None),
        P(),
        P(),
        P(),
    )
    return jax.shard_map(
        shards, mesh=mesh, in_specs=placed, out_specs=P("sec", None, None), check_vma=False
    )
```

profile of v0, /device:TPU:1, one launch (start us, length us, event | category | flops | bytes accessed | tf_op | source)
XLA Modules:
  0.0 491.5 jit_solution(16552555953608625881)
XLA Ops:
  6.5 0.7 all-gather.4.cloned.1.call-update
  7.3 1.4 fusion.32
  12.5 1.3 fusion.33
  16.4 2.7 slice_bitcast_fusion
  19.1 0.4 copy.24
  19.4 3.0 slice_bitcast_fusion.1
  22.5 1.2 copy.23
  23.6 7.8 %convert_bitcast_fusion.2 = bf16[32,32,32,32]{1,0,3,2:T(8,128)(2,1)} fusion(bf16[32,32,384,1]{2,1,3,0:T(8,128)(2,1)} %bitcast.124, bf16[32,32,384,1]{2,1,0,3:T(8,128)(2,1)S(1)} %bitcast.121), kind=kOutput, calls=%fused_computation.4 | convolution fusion | flops 806354944 | bytes 3670016 | tf_op jit(solution)/shard_map/dot_general | solution.py:11
  31.5 11.3 %convert_element_type.51 = bf16[1024,1024]{0,1:T(8,128)(2,1)S(1)} reshape(bf16[32,32,32,32]{1,0,3,2:T(8,128)(2,1)} %convert_bitcast_fusion.2) | data formatting | bytes 4194304 | tf_op jit(solution)/shard_map/convert_element_type | solution.py:15
  42.8 2.3 copy.25
  45.1 2.3 copy.26
  47.4 7.9 %convert_bitcast_fusion.1 = bf16[32,32,32,32]{1,0,3,2:T(8,128)(2,1)} fusion(bf16[32,32,384,1]{2,1,3,0:T(8,128)(2,1)} %bitcast.123, bf16[32,32,384,1]{2,1,0,3:T(8,128)(2,1)} %bitcast.125), kind=kOutput, calls=%fused_computation.3 | convolution fusion | flops 806354944 | bytes 3670016 | tf_op jit(solution)/shard_map/dot_general | solution.py:11
  55.4 12.4 %convert_element_type.54 = bf16[1024,1024]{0,1:T(8,128)(2,1)} reshape(bf16[32,32,32,32]{1,0,3,2:T(8,128)(2,1)} %convert_bitcast_fusion.1) | data formatting | bytes 4194304 | tf_op jit(solution)/shard_map/convert_element_type | solution.py:15
  67.8 2.3 copy.27
  70.1 1.2 copy.28
  71.3 7.9 %convert_bitcast_fusion = bf16[32,32,32,32]{1,0,3,2:T(8,128)(2,1)} fusion(bf16[32,32,384,1]{2,1,3,0:T(8,128)(2,1)} %bitcast.122, bf16[32,32,384,1]{2,1,0,3:T(8,128)(2,1)} %bitcast.126), kind=kOutput, calls=%fused_computation.2 | convolution fusion | flops 806354944 | bytes 3670016 | tf_op jit(solution)/shard_map/dot_general | solution.py:11
  79.2 12.4 %convert_element_type.57 = bf16[1024,1024]{0,1:T(8,128)(2,1)} reshape(bf16[32,32,32,32]{1,0,3,2:T(8,128)(2,1)} %convert_bitcast_fusion) | data formatting | bytes 4194304 | tf_op jit(solution)/shard_map/convert_element_type | solution.py:15
  95.2 0.7 fusion.31
  95.9 64.5 %all-gather.4.cloned.1.call-done = bf16[64,16,1024]{2,1,0:T(8,128)(2,1)} async-done(((bf16[1,16,1024]{2,1,0:T(8,128)(2,1)}), bf16[64,16,1024]{2,1,0:T(8,128)(2,1)}) %all-gather.4.cloned.1.call-update) | async-done | bytes 2097168 | tf_op jit(solution)/shard_map/all_gather | solution.py:45
  160.4 2.6 convolution_multiply_fusion.5
  162.9 2.0 fusion.3
  165.0 2.7 fusion.2
  167.8 0.7 gather_fusion
  168.4 0.7 gather_fusion.1
  169.1 76.7 %all-reduce.3.cloned.1.call-done = f32[16,1024]{1,0:T(8,128)} async-done(((f32[16,1024]{1,0:T(8,128)}), f32[16,1024]{1,0:T(8,128)}) %all-reduce.3.cloned.1.call-update) | async-done | bytes 65552 | tf_op jit(solution)/shard_map/psum | solution.py:50
  245.9 1.5 fusion.6
  247.5 150.4 %all-gather.6.cloned.1.call-done = bf16[1024,1024]{1,0:T(8,128)(2,1)} async-done(((bf16[16,1024]{1,0:T(8,128)(2,1)}), bf16[1024,1024]{1,0:T(8,128)(2,1)}) %all-gather.6.cloned.1.call-update) | async-done | bytes 2097168 | tf_op jit(solution)/shard_map/all_gather | solution.py:53
  397.9 2.6 convolution_multiply_fusion.2
  400.5 2.0 fusion.1
  402.5 2.8 fusion
  405.3 78.2 %all-reduce.5.cloned.1.call-done = f32[16,1024]{1,0:T(8,128)} async-done(((f32[16,1024]{1,0:T(8,128)}), f32[16,1024]{1,0:T(8,128)}) %all-reduce.5.cloned.1.call-update) | async-done | bytes 65552 | tf_op jit(solution)/shard_map/psum | solution.py:50
  483.4 1.5 fusion.20
  (36 shorter events, 0.6 us)
Async XLA Ops:
  6.5 161.2 %copy-start = (f32[128]{0:T(128)S(1)}, f32[128]{0:T(128)}, u32[]{:S(2)}) copy-start(f32[128]{0:T(128)} %param.19) | copy-start | bytes 1540
  6.5 153.8 %all-gather.4.cloned.1.call-start = ((), (), s32[]{:S(2)}) async-start(), calls=%async_computation | async-start | bytes 2129920 | tf_op jit(solution)/shard_map/all_gather | solution.py:45
  7.3 238.6 %all-reduce.3.cloned.1.call-start = ((), (), s32[]{:S(2)}) async-start(), calls=%async_computation.1 | async-start | bytes 131072 | tf_op jit(solution)/shard_map/psum | solution.py:50
  31.5 11.3 %copy-start.8 = (s32[1,3]{1,0:T(1,128)S(1)}, s32[1,3]{1,0:T(1,128)}, u32[]{:S(2)}) copy-start(s32[1,3]{1,0:T(1,128)} %param.15) | copy-start | bytes 40
  79.2 12.4 %copy-start.6 = (f32[1024]{0:T(1024)S(1)}, f32[1024]{0:T(1024)}, u32[]{:S(2)}) copy-start(f32[1024]{0:T(1024)} %param.18) | copy-start | bytes 12292
  79.2 16.7 %copy-start.7 = (s32[16,2]{0,1:T(2,128)S(1)}, s32[16,2]{0,1:T(2,128)}, u32[]{:S(2)}) copy-start(s32[16,2]{0,1:T(2,128)} %param.17) | copy-start | bytes 388
  160.4 2.6 copy-start.1
  160.4 4.6 copy-start.3
  164.9 80.9 %copy-start.5 = (bf16[1,16,1024]{2,1,0:T(8,128)(2,1)S(1)}, bf16[1,16,1024]{2,1,0:T(8,128)(2,1)}, u32[]{:S(2)}) copy-start(bf16[1,16,1024]{2,1,0:T(8,128)(2,1)} %param.11) | copy-start | bytes 98308
  167.7 230.2 %all-gather.6.cloned.1.call-start = ((), (), s32[]{:S(2)}) async-start(), calls=%async_computation.3 | async-start | bytes 2129920 | tf_op jit(solution)/shard_map/all_gather | solution.py:53
  247.4 236.0 %all-reduce.5.cloned.1.call-start = ((), (), s32[]{:S(2)}) async-start(), calls=%async_computation.2 | async-start | bytes 131072 | tf_op jit(solution)/shard_map/psum | solution.py:50
  397.9 2.6 copy-start.2
  397.9 4.6 copy-start.4
Sparse Core Ops, SparseCore 0:
  10.6 149.7 all-gather.3
  167.8 77.9 all-reduce.2
  249.2 148.7 all-gather.5
  405.4 77.9 all-reduce.4
where the time goes:
time: 497 us; the launch traced here: 491 us
  waiting for transfers between devices  371 us (75%)
  local copies, waits for them, and re-layouts  56.7 us (11%)
  matrix products  38.3 us (8%)
  between operations  22.7 us (5%)
    psum x2, waiting for transfers between devices, shards(): summed = lax.psum(local_sum, 'chol')  155 us
    all_gather x1, waiting for transfers between devices, shards(): every = lax.all_gather(current, 'sec', axis=0, tiled=True)  150 us
    all_gather x1, waiting for transfers between devices, shards(): every = lax.all_gather(amplitudes, 'sec', axis=0, tiled=True)  64.5 us
    convert_element_type x3, local copies, waits for them, and re-layouts, integral(): return product.reshape(TS * TS, TS * TS).astype(jnp.bfloat16)  36.2 us
    dot_general x3, matrix products, integral(): lax.dot_general(left_tile, right_tile, (((0,), (0,)), ((), ())), preferre...  23.7 us
    dot_general x8, local copies, waits for them, and re-layouts, integral(): lax.dot_general(left_tile, right_tile, (((0,), (0,)), ((), ())), preferre...  15.3 us
    dot_general x6, matrix products, ladder(): jnp.dot(picked, cached[slot_idx], preferred_element_type=jnp.float32)  14.6 us
  transfers between devices with their start and end apart: 4, of which 4 were waited for; matrix products, arithmetic and copies ran while one was open for 16% of the time, Pallas kernels for 0%

commit v1 on v0

v1 whole, which is shorter than its diff:
```python
import jax
import jax.numpy as jnp
from jax import lax
from jax.experimental import pallas as pl
from jax.experimental.pallas import tpu as pltpu
from jax.sharding import PartitionSpec as P

TS = 32
TT = TS * TS
ROWS = 16
SLOTS = 3
DEPTH = 384
NSEC = 64
NCHIP = 32
NCHOL = 8
LANES = 128
MESH = pl.DeviceIdType.MESH
F32 = jnp.float32
BF16 = jnp.bfloat16


def mod(value, size):
    return lax.rem(value + size, size)


def build_column_order(order):
    for part in range(4):
        row = lax.broadcasted_iota(jnp.int32, (256, TT), 0) + part * 256
        col = lax.broadcasted_iota(jnp.int32, (256, TT), 1)
        want = (row & 7) * 128 + ((row >> 3) & 3) * 32 + (row >> 5)
        order[part * 256 : part * 256 + 256, :] = jnp.where(col == want, 1.0, 0.0).astype(BF16)


def build_swap(swap):
    for part in range(4):
        row = lax.broadcasted_iota(jnp.int32, (256, TT), 0) + part * 256
        col = lax.broadcasted_iota(jnp.int32, (256, TT), 1)
        want = (row & 31) * 32 + (row >> 5)
        swap[part * 256 : part * 256 + 256, :] = jnp.where(col == want, 1.0, 0.0).astype(BF16)


def build_integral(slot, xv, yv, order, xp, vs):
    xp[...] = jnp.dot(xv[slot], order[...], preferred_element_type=F32).astype(BF16)

    def chunk(part, carry):
        right = yv[slot, :, pl.ds(pl.multiple_of(part * 256, 256), 256)]
        block = lax.dot_general(
            right, xp[...], (((0,), (0,)), ((), ())), preferred_element_type=F32
        ).astype(BF16)
        for e in range(8):
            for c in range(8):
                column = pl.multiple_of(part * 1024 + e * 128, 128)
                vs[slot, c * 32 : c * 32 + 32, pl.ds(column, 128)] = block[
                    e * 32 : e * 32 + 32, c * 128 : c * 128 + 128
                ]
        return carry

    lax.fori_loop(0, 4, chunk, 0)


def kernel(
    sources, live, tiles, pairs, e_virt, e_occ, amp, drv, x_hbm, y_hbm, out,
    xv, yv, order, swap, xp, vs, left, stack, first, second, picked, part, sums, driven, final,
    load_sem, ag_send, ag_recv, fw_send, fw_recv, pk_send, pk_recv, rs_send, rs_recv,
    fin_send, fin_recv,
):
    sec = lax.axis_index("sec")
    chol = lax.axis_index("chol")
    chip = sec // 2
    core = sec - 2 * chip
    x_hi = chip // 16
    z = chip - 16 * x_hi
    other = 2 * chip + 1 - core
    blocks = (first, second)

    loads = []
    for slot in range(SLOTS):
        pair = (
            pltpu.make_async_copy(x_hbm.at[0, slot], xv.at[slot], load_sem.at[slot]),
            pltpu.make_async_copy(y_hbm.at[0, slot], yv.at[slot], load_sem.at[SLOTS + slot]),
        )
        for copy in pair:
            copy.start()
        loads.append(pair)

    def far_chip(step):
        turn = step // 2
        away = 8 + (1 - 2 * lax.rem(turn, 2)) * ((turn + 1) // 2)
        side = 1 - lax.rem(step, 2)
        return lax.rem(x_hi + side, 2) * 16 + lax.rem(z + away, 16)

    barrier = pltpu.get_barrier_semaphore()

    def greet(step, carry):
        pl.semaphore_signal(
            barrier, inc=1, device_id=(2 * far_chip(step) + core, chol), device_id_type=MESH
        )
        return carry

    lax.fori_loop(0, NCHIP - 1, greet, 0)

    def greet_chol(step, carry):
        pl.semaphore_signal(
            barrier, inc=1, device_id=(sec, lax.rem(chol + step, NCHOL)), device_id_type=MESH
        )
        return carry

    lax.fori_loop(1, NCHOL, greet_chol, 0)
    pl.semaphore_signal(barrier, inc=1, device_id=(other, chol), device_id_type=MESH)

    def gather_copy(turn, step):
        return pltpu.make_async_remote_copy(
            src_ref=blocks[turn].at[sec],
            dst_ref=blocks[turn].at[sec],
            send_sem=ag_send.at[turn, step],
            recv_sem=ag_recv.at[turn, chip],
            device_id=(2 * far_chip(step) + core, chol),
            device_id_type=MESH,
        )

    def gather_arrival(turn, step):
        source = far_chip(step)
        return pltpu.make_async_remote_copy(
            src_ref=blocks[turn].at[sec],
            dst_ref=blocks[turn].at[2 * source + core],
            send_sem=ag_send.at[turn, step],
            recv_sem=ag_recv.at[turn, source],
            device_id=(2 * source + core, chol),
            device_id_type=MESH,
        )

    def forward_copy(turn, source):
        return pltpu.make_async_remote_copy(
            src_ref=blocks[turn].at[2 * source + core],
            dst_ref=blocks[turn].at[2 * source + core],
            send_sem=fw_send.at[turn, source],
            recv_sem=fw_recv.at[turn, source],
            device_id=(other, chol),
            device_id_type=MESH,
        )

    def forward_arrival(turn, source):
        return pltpu.make_async_remote_copy(
            src_ref=blocks[turn].at[2 * source + core],
            dst_ref=blocks[turn].at[2 * source + 1 - core],
            send_sem=fw_send.at[turn, source],
            recv_sem=fw_recv.at[turn, source],
            device_id=(other, chol),
            device_id_type=MESH,
        )

    def gather_start(turn):
        def send(step, carry):
            gather_copy(turn, step).start()
            return carry

        lax.fori_loop(0, NCHIP - 1, send, 0)
        forward_copy(turn, chip).start()

    def gather_finish(turn):
        def take(step, carry):
            back = NCHIP - 2 - step
            gather_arrival(turn, back).wait_recv()
            forward_copy(turn, far_chip(back)).start()
            return carry

        lax.fori_loop(0, NCHIP - 1, take, 0)

        def settle(source, carry):
            forward_arrival(turn, source).wait_recv()
            return carry

        lax.fori_loop(0, NCHIP, settle, 0)

    def gather_drain(turn):
        def drain(step, carry):
            gather_copy(turn, step).wait_send()
            return carry

        lax.fori_loop(0, NCHIP - 1, drain, 0)

        def drain_forward(source, carry):
            forward_copy(turn, source).wait_send()
            return carry

        lax.fori_loop(0, NCHIP, drain_forward, 0)

    def pick_copy(turn, slot_from, peer):
        return pltpu.make_async_remote_copy(
            src_ref=picked.at[turn, chol],
            dst_ref=picked.at[turn, slot_from],
            send_sem=pk_send.at[turn, peer],
            recv_sem=pk_recv.at[turn, slot_from],
            device_id=(sec, peer),
            device_id_type=MESH,
        )

    def share_picks(turn):
        for slot in range(SLOTS):
            chosen = blocks[turn][sources[0, slot]].astype(F32)
            picked[turn, chol, slot] = (chosen * live[0, slot].astype(F32)).astype(BF16)

        def send(step, carry):
            pick_copy(turn, chol, lax.rem(chol + step, NCHOL)).start()
            return carry

        lax.fori_loop(1, NCHOL, send, 0)

        def take(step, carry):
            peer = lax.rem(chol + step, NCHOL)
            pick_copy(turn, peer, peer).wait_recv()
            return carry

        lax.fori_loop(1, NCHOL, take, 0)

    def drain_picks(turn):
        def drain(step, carry):
            pick_copy(turn, chol, lax.rem(chol + step, NCHOL)).wait_send()
            return carry

        lax.fori_loop(1, NCHOL, drain, 0)

    def sum_copy(turn, slot_from, peer):
        return pltpu.make_async_remote_copy(
            src_ref=part.at[turn, peer],
            dst_ref=sums.at[turn, slot_from],
            send_sem=rs_send.at[turn, peer],
            recv_sem=rs_recv.at[turn, slot_from],
            device_id=(sec, peer),
            device_id_type=MESH,
        )

    group = lax.broadcasted_iota(jnp.int32, (ROWS, LANES), 1) >> 5

    def ladder(turn):
        for j in range(NCHOL):
            total = jnp.zeros((4 * ROWS, 4 * LANES), F32)
            for slot in range(SLOTS):
                total += jnp.dot(
                    left[slot], vs[slot, :, j * 512 : j * 512 + 512], preferred_element_type=F32
                )
            joined = None
            for g in range(4):
                block = total[:, g * LANES : g * LANES + LANES]
                own = block[3 * ROWS : 4 * ROWS]
                for w in range(3):
                    own = jnp.where(group == w, block[w * ROWS : w * ROWS + ROWS], own)
                own = own + pltpu.roll(own, 64, 1)
                own = own + pltpu.roll(own, 32, 1)
                joined = own if g == 0 else jnp.where(group == g, own, joined)
            part[turn, j] = joined

    def reduce(turn):
        def send(step, carry):
            sum_copy(turn, chol, lax.rem(chol + step, NCHOL)).start()
            return carry

        lax.fori_loop(1, NCHOL, send, 0)
        sums[turn, chol] = part[turn, chol]

        def take(step, carry):
            peer = lax.rem(chol + step, NCHOL)
            sum_copy(turn, peer, peer).wait_recv()
            return carry

        lax.fori_loop(1, NCHOL, take, 0)
        total = sums[turn, 0]
        for j in range(1, NCHOL):
            total = total + sums[turn, j]
        return total

    def drain_sums(turn):
        def drain(step, carry):
            sum_copy(turn, chol, lax.rem(chol + step, NCHOL)).wait_send()
            return carry

        lax.fori_loop(1, NCHOL, drain, 0)

    def final_copy(slot_from, peer):
        return pltpu.make_async_remote_copy(
            src_ref=final.at[chol],
            dst_ref=final.at[slot_from],
            send_sem=fin_send.at[peer],
            recv_sem=fin_recv.at[slot_from],
            device_id=(sec, peer),
            device_id_type=MESH,
        )

    build_column_order(order)
    for copy in loads[0]:
        copy.wait()
    build_integral(0, xv, yv, order, xp, vs)

    first[sec] = amp[0, :, pl.ds(pl.multiple_of(chol * LANES, LANES), LANES)]
    pl.semaphore_wait(barrier, NCHIP - 1 + NCHOL - 1 + 1)
    gather_start(0)

    for slot in range(1, SLOTS):
        for copy in loads[slot]:
            copy.wait()
        build_integral(slot, xv, yv, order, xp, vs)

    build_swap(swap)
    turned = jnp.dot(drv[0], swap[...], preferred_element_type=F32)
    for j in range(NCHOL):
        driven[j] = turned[:, j * LANES : j * LANES + LANES]
    lane = lax.broadcasted_iota(jnp.int32, (1, LANES), 1)
    energy_a = jnp.zeros((1, LANES), F32)
    for a in range(TS):
        energy_a = jnp.where((lane & 31) == a, e_virt[TS * tiles[0, 0] + a], energy_a)
    energy_b = jnp.zeros((1, LANES), F32)
    for e in range(4):
        energy_b = jnp.where((lane >> 5) == e, e_virt[TS * tiles[0, 1] + 4 * chol + e], energy_b)
    row = lax.broadcasted_iota(jnp.int32, (ROWS, LANES), 0)
    energy_ij = jnp.zeros((ROWS, LANES), F32)
    for p in range(ROWS):
        energy_ij = jnp.where(row == p, e_occ[pairs[0, p]] + e_occ[pairs[1, p]], energy_ij)
    denominator = (energy_a + energy_b) - energy_ij
    own_driven = driven[chol]

    gather_finish(0)
    share_picks(0)
    for slot in range(SLOTS):
        for j in range(NCHOL):
            w, h = j // 2, j % 2
            left[slot, w * ROWS : w * ROWS + ROWS, h * LANES : h * LANES + LANES] = picked[0, j, slot]
    ladder(0)
    second[sec] = (-(own_driven + reduce(0)) / denominator).astype(BF16)
    gather_start(1)
    gather_finish(1)
    share_picks(1)
    for slot in range(SLOTS):
        for j in range(NCHOL):
            stack[slot * ROWS : slot * ROWS + ROWS, j * LANES : j * LANES + LANES] = picked[1, j, slot]
    turned = jnp.dot(stack[...], swap[...], preferred_element_type=F32).astype(BF16)
    for slot in range(SLOTS):
        for w in range(4):
            left[slot, w * ROWS : w * ROWS + ROWS, :] = turned[
                slot * ROWS : slot * ROWS + ROWS, w * 256 : w * 256 + 256
            ]
    ladder(1)
    final[chol] = (-(own_driven + reduce(1)) / denominator).astype(BF16)

    def send_final(step, carry):
        final_copy(chol, lax.rem(chol + step, NCHOL)).start()
        return carry

    lax.fori_loop(1, NCHOL, send_final, 0)

    def take_final(step, carry):
        peer = lax.rem(chol + step, NCHOL)
        final_copy(peer, peer).wait_recv()
        return carry

    lax.fori_loop(1, NCHOL, take_final, 0)
    for j in range(NCHOL):
        stack[0:ROWS, j * LANES : j * LANES + LANES] = final[j]
    out[0] = jnp.dot(stack[0:ROWS, :], swap[...], preferred_element_type=F32).astype(BF16)

    for turn in range(2):
        gather_drain(turn)
        drain_picks(turn)
        drain_sums(turn)

    def drain_final(step, carry):
        final_copy(chol, lax.rem(chol + step, NCHOL)).wait_send()
        return carry

    lax.fori_loop(1, NCHOL, drain_final, 0)


def shards(amplitudes, driver, x_tiles, y_tiles, sources, live, block_tiles, pairs, e_virt, e_occ):
    smem = pl.BlockSpec(memory_space=pltpu.SMEM)
    vmem = pl.BlockSpec(memory_space=pltpu.VMEM)
    hbm = pl.BlockSpec(memory_space=pl.ANY)
    dma = pltpu.SemaphoreType.DMA
    return pl.pallas_call(
        kernel,
        out_shape=jax.ShapeDtypeStruct((1, ROWS, TT), BF16),
        in_specs=[smem] * 6 + [vmem, vmem, hbm, hbm],
        out_specs=vmem,
        scratch_shapes=[
            pltpu.VMEM((SLOTS, DEPTH, TT), BF16),
            pltpu.VMEM((SLOTS, DEPTH, TT), BF16),
            pltpu.VMEM((TT, TT), BF16),
            pltpu.VMEM((TT, TT), BF16),
            pltpu.VMEM((DEPTH, TT), BF16),
            pltpu.VMEM((SLOTS, 256, 4096), BF16),
            pltpu.VMEM((SLOTS, 4 * ROWS, 256), BF16),
            pltpu.VMEM((SLOTS * ROWS, TT), BF16),
            pltpu.VMEM((NSEC, ROWS, LANES), BF16),
            pltpu.VMEM((NSEC, ROWS, LANES), BF16),
            pltpu.VMEM((2, NCHOL, SLOTS, ROWS, LANES), BF16),
            pltpu.VMEM((2, NCHOL, ROWS, LANES), F32),
            pltpu.VMEM((2, NCHOL, ROWS, LANES), F32),
            pltpu.VMEM((NCHOL, ROWS, LANES), F32),
            pltpu.VMEM((NCHOL, ROWS, LANES), BF16),
            dma((2 * SLOTS,)),
            dma((2, NCHIP)),
            dma((2, NCHIP)),
            dma((2, NCHIP)),
            dma((2, NCHIP)),
            dma((2, NCHOL)),
            dma((2, NCHOL)),
            dma((2, NCHOL)),
            dma((2, NCHOL)),
            dma((NCHOL,)),
            dma((NCHOL,)),
        ],
        compiler_params=pltpu.CompilerParams(
            collective_id=0, has_side_effects=True, vmem_limit_bytes=67043328
        ),
        name="ladder_sweeps",
    )(sources, live, block_tiles, pairs.T, e_virt, e_occ, amplitudes, driver, x_tiles, y_tiles)


def solution(mesh):
    placed = (
        P("sec", None, None),
        P("sec", None, None),
        P("sec", None, "chol", None),
        P("sec", None, "chol", None),
        P("sec", None),
        P("sec", None),
        P("sec", None),
        P(),
        P(),
        P(),
    )
    return jax.shard_map(
        shards, mesh=mesh, in_specs=placed, out_specs=P("sec", None, None), check_vma=False
    )
```

time: 497 us -> 68.6 us (0.14); the launches traced: 491 us -> 68.2 us
  waiting for transfers between devices: 371 us -> 0 us
  Pallas kernels: 0 us -> 66.8 us
  local copies, waits for them, and re-layouts: 56.7 us -> 1.38 us
  matrix products: 38.3 us -> 0 us
  between operations: 22.7 us -> 0.01 us
    all_gather x2 -> x0, waiting for transfers between devices: 215 us -> none  [the longest x1 150 us: shards(): every = lax.all_gather(current, 'sec', axis=0, tiled=True)]
    psum x2 -> x0, waiting for transfers between devices: 155 us -> none  [shards(): summed = lax.psum(local_sum, 'chol')]
    pallas_call x0 -> x1, Pallas kernels: none -> 66.8 us  [shards(): pl.pallas_call(kernel, out_shape=jax.ShapeDtypeStruct((1, ROWS, TT), BF16...]
    dot_general x9 -> x0, matrix products: 38.3 us -> none  [the longest x3 23.7 us: integral(): lax.dot_general(left_tile, right_tile, (((0,), (0,)), ((), ())), preferre...]
    convert_element_type x3 -> x0, local copies, waits for them, and re-layouts: 36.2 us -> none  [integral(): return product.reshape(TS * TS, TS * TS).astype(jnp.bfloat16)]
    dot_general x8 -> x0, local copies, waits for them, and re-layouts: 15.3 us -> none  [integral(): lax.dot_general(left_tile, right_tile, (((0,), (0,)), ((), ())), preferre...]
  transfers between devices with their start and end apart: 4 -> 0, of which waited for: 4 -> 0; matrix products, arithmetic and copies ran while one was open for 16% -> 0% of each run, Pallas kernels for 0% -> 0%
where the time goes in v1:
time: 68.6 us; the launch traced here: 68.2 us
  Pallas kernels  66.8 us (97%)
  local copies, waits for them, and re-layouts  1.38 us (2%)
    pallas_call x1, Pallas kernels, shards(): pl.pallas_call(kernel, out_shape=jax.ShapeDtypeStruct((1, ROWS, TT), BF16...  66.8 us
    unnamed x1, local copies, waits for them, and re-layouts  1.38 us

profile of v1, /device:TPU:1, one launch (start us, length us, event | category | flops | bytes accessed | tf_op | source)
XLA Modules:
  0.0 68.2 jit_solution(13298707783026646713)
XLA Ops:
  0.0 66.8 %ladder_sweeps.1 = bf16[1,16,1024]{2,1,0:T(8,128)(2,1)} custom-call(s32[1,3]{1,0:T(1,128)} %sources.1, s32[1,3]{1,0:T(1,128)} %live.1, s32[1,2]{1,0:T(1,128)} %tiles.1, s32[2,16]{1,0:T(2,128)} %bitcast.1, f32[1024]{0:T(1024)} %e_virt.1, f32[128]{0:T(128)} %e_occ.1, bf16[1,16,1024]{2,1,0:T(8,128)(2,1)} %amp.1, bf16[1,16,1024]{2,1,0:T(8,128)(2,1)} %drv.1, ...), custom_call_target="tpu_custom_call" | custom-call | tf_op jit(solution)/shard_map/ladder_sweeps/pallas_call | solution.py:377
  66.8 1.4 %copy.12 = bf16[1,16,1024]{2,1,0:T(8,128)(2,1)} copy(bf16[1,16,1024]{2,1,0:T(8,128)(2,1)} %ladder_sweeps.1) | data formatting | bytes 65536

commit v2 on v0

v2 whole, which is shorter than its diff:
```python
import jax
import jax.numpy as jnp
from jax import lax
from jax.experimental import pallas as pl
from jax.experimental.pallas import tpu as pltpu
from jax.sharding import PartitionSpec as P

TS = 32
TT = TS * TS
ROWS = 16
SLOTS = 3
DEPTH = 384
NCHIP = 32
NPAIR = 16
NCHOL = 8
LANES = 128
MESH = pl.DeviceIdType.MESH
F32 = jnp.float32
BF16 = jnp.bfloat16


def build_column_order(order):
    for part in range(4):
        row = lax.broadcasted_iota(jnp.int32, (256, TT), 0) + part * 256
        col = lax.broadcasted_iota(jnp.int32, (256, TT), 1)
        want = (row & 7) * 128 + ((row >> 3) & 3) * 32 + (row >> 5)
        order[part * 256 : part * 256 + 256, :] = jnp.where(col == want, 1.0, 0.0).astype(BF16)


def build_swap(swap):
    for part in range(4):
        row = lax.broadcasted_iota(jnp.int32, (256, TT), 0) + part * 256
        col = lax.broadcasted_iota(jnp.int32, (256, TT), 1)
        want = (row & 31) * 32 + (row >> 5)
        swap[part * 256 : part * 256 + 256, :] = jnp.where(col == want, 1.0, 0.0).astype(BF16)


def build_integral(slot, xv, yv, order, xp, vs):
    xp[...] = jnp.dot(xv[slot], order[...], preferred_element_type=F32).astype(BF16)

    def chunk(part, carry):
        right = yv[slot, :, pl.ds(pl.multiple_of(part * 256, 256), 256)]
        block = lax.dot_general(
            right, xp[...], (((0,), (0,)), ((), ())), preferred_element_type=F32
        ).astype(BF16)
        for e in range(8):
            for c in range(8):
                column = pl.multiple_of(part * 1024 + e * 128, 128)
                vs[slot, c * 32 : c * 32 + 32, pl.ds(column, 128)] = block[
                    e * 32 : e * 32 + 32, c * 128 : c * 128 + 128
                ]
        return carry

    lax.fori_loop(0, 4, chunk, 0)


def kernel(
    sources_hbm, live_hbm, tiles_hbm, pairs_hbm, e_virt_hbm, e_occ_hbm, amp_hbm, drv_hbm, x_hbm,
    y_hbm, out,
    sources, live, tiles, pairs, e_virt, e_occ, amp, drv, xv, yv, order, swap, xp, vs, left, stack, wishes, blocks, offers, picked, part, sums,
    driven, denominator, final,
    small_sem, load_sem, wish_send, wish_recv, ag_send, ag_recv, pk_send, pk_recv, rs_send, rs_recv,
    fin_send, fin_recv,
):
    sec = lax.axis_index("sec")
    chol = lax.axis_index("chol")
    chip = sec // 2
    core = sec - 2 * chip
    x_hi = chip // 16
    z = chip - 16 * x_hi
    other = 2 * chip + 1 - core

    def far_chip(step):
        turn = step // 2
        away = 8 + (1 - 2 * lax.rem(turn, 2)) * ((turn + 1) // 2)
        side = 1 - lax.rem(step, 2)
        return lax.rem(x_hi + side, 2) * 16 + lax.rem(z + away, 16)

    def near_core(step):
        return lax.rem(core + lax.rem(step, 2), 2)

    def near_chol(step):
        return lax.rem(chol + step // 2, NCHOL)

    def near(step):
        return (2 * chip + near_core(step), near_chol(step))

    barrier = pltpu.get_barrier_semaphore()

    def greet(step, carry):
        pl.semaphore_signal(
            barrier, inc=1, device_id=(2 * far_chip(step) + core, chol), device_id_type=MESH
        )
        return carry

    lax.fori_loop(0, NCHIP - 1, greet, 0)

    def greet_near(step, carry):
        pl.semaphore_signal(barrier, inc=1, device_id=near(step), device_id_type=MESH)
        return carry

    lax.fori_loop(1, NPAIR, greet_near, 0)

    small = [
        pltpu.make_async_copy(source, target, small_sem.at[place])
        for place, (source, target) in enumerate(
            (
                (amp_hbm, amp),
                (sources_hbm, sources),
                (live_hbm, live),
                (drv_hbm, drv),
                (tiles_hbm, tiles),
                (pairs_hbm, pairs),
                (e_virt_hbm, e_virt),
                (e_occ_hbm, e_occ),
            )
        )
    ]
    for copy in small:
        copy.start()
    loads = []
    for slot in range(SLOTS):
        pair = (
            pltpu.make_async_copy(x_hbm.at[0, slot], xv.at[slot], load_sem.at[slot]),
            pltpu.make_async_copy(y_hbm.at[0, slot], yv.at[slot], load_sem.at[SLOTS + slot]),
        )
        for copy in pair:
            copy.start()
        loads.append(pair)

    def wish_copy(half):
        return pltpu.make_async_remote_copy(
            src_ref=wishes.at[core],
            dst_ref=wishes.at[half],
            send_sem=wish_send,
            recv_sem=wish_recv,
            device_id=(other, chol),
            device_id_type=MESH,
        )

    def gather_copy(turn, slot_from, step):
        return pltpu.make_async_remote_copy(
            src_ref=blocks.at[turn, chip],
            dst_ref=blocks.at[turn, slot_from],
            send_sem=ag_send.at[turn, step],
            recv_sem=ag_recv.at[turn, slot_from],
            device_id=(2 * far_chip(step) + core, chol),
            device_id_type=MESH,
        )

    def gather_start(turn):
        def send(step, carry):
            gather_copy(turn, chip, step).start()
            return carry

        lax.fori_loop(0, NCHIP - 1, send, 0)

    def pick_copy(turn, half, column, step):
        return pltpu.make_async_remote_copy(
            src_ref=offers.at[turn, near_core(step)],
            dst_ref=picked.at[turn, half, column],
            send_sem=pk_send.at[turn, step],
            recv_sem=pk_recv.at[turn, half, column],
            device_id=near(step),
            device_id_type=MESH,
        )

    def share_picks(turn):
        def take_block(step, carry):
            gather_copy(turn, far_chip(step), step).wait_recv()
            return carry

        lax.fori_loop(0, NCHIP - 1, take_block, 0)
        asked = [
            jnp.broadcast_to(wishes[half, slot : slot + 1, :], (ROWS, LANES))
            for half in range(2)
            for slot in range(SLOTS)
        ]

        def look(source, found):
            block = blocks[turn, source].astype(F32)
            name = (2 * source + core).astype(F32)
            return tuple(jnp.where(a == name, block, f) for a, f in zip(asked, found))

        found = lax.fori_loop(0, NCHIP, look, (jnp.zeros((ROWS, LANES), F32),) * (2 * SLOTS))
        for half in range(2):
            for slot in range(SLOTS):
                offers[turn, half, slot] = found[SLOTS * half + slot].astype(BF16)

        def send(step, carry):
            pick_copy(turn, core, chol, step).start()
            return carry

        lax.fori_loop(1, NPAIR, send, 0)
        picked[turn, core, chol] = offers[turn, core]

        def take(step, carry):
            pick_copy(turn, near_core(step), near_chol(step), step).wait_recv()
            return carry

        lax.fori_loop(1, NPAIR, take, 0)

    def share_drain(turn):
        def drain_block(step, carry):
            gather_copy(turn, chip, step).wait_send()
            return carry

        lax.fori_loop(0, NCHIP - 1, drain_block, 0)

        def drain(step, carry):
            pick_copy(turn, core, chol, step).wait_send()
            return carry

        lax.fori_loop(1, NPAIR, drain, 0)

    def arrived(turn, j, slot):
        return picked[turn, 0, j, slot] + picked[turn, 1, j, slot]

    def sum_copy(slot_from, peer):
        return pltpu.make_async_remote_copy(
            src_ref=part.at[peer],
            dst_ref=sums.at[slot_from],
            send_sem=rs_send.at[peer],
            recv_sem=rs_recv.at[slot_from],
            device_id=(sec, peer),
            device_id_type=MESH,
        )

    def final_copy(half, slot_from, peer):
        return pltpu.make_async_remote_copy(
            src_ref=final.at[half, chol],
            dst_ref=final.at[half, slot_from],
            send_sem=fin_send.at[half, peer],
            recv_sem=fin_recv.at[half, slot_from],
            device_id=(sec, peer),
            device_id_type=MESH,
        )

    group = lax.broadcasted_iota(jnp.int32, (ROWS, LANES), 1) >> 5

    def ladder(j):
        total = jnp.zeros((4 * ROWS, 4 * LANES), F32)
        for slot in range(SLOTS):
            columns = vs[slot, :, pl.ds(pl.multiple_of(j * 512, 512), 512)]
            total += jnp.dot(left[slot], columns, preferred_element_type=F32)
        joined = None
        for g in range(4):
            block = total[:, g * LANES : g * LANES + LANES]
            own = block[3 * ROWS : 4 * ROWS]
            for w in range(3):
                own = jnp.where(group == w, block[w * ROWS : w * ROWS + ROWS], own)
            own = own + pltpu.roll(own, 64, 1)
            own = own + pltpu.roll(own, 32, 1)
            joined = own if g == 0 else jnp.where(group == g, own, joined)
        return joined

    build_column_order(order)
    for copy in small:
        copy.wait()
    for copy in loads[0]:
        copy.wait()
    build_integral(0, xv, yv, order, xp, vs)

    blocks[0, chip] = amp[0, :, pl.ds(pl.multiple_of(chol * LANES, LANES), LANES)]
    asking = jnp.full((8, LANES), -1.0, F32)
    ask_row = lax.broadcasted_iota(jnp.int32, (8, LANES), 0)
    for slot in range(SLOTS):
        wish = (sources[0, slot] + 1) * live[0, slot] - 1
        asking = jnp.where(ask_row == slot, wish.astype(F32), asking)
    wishes[core] = asking
    pl.semaphore_wait(barrier, NCHIP - 1 + NPAIR - 1)
    gather_start(0)

    wish_copy(core).start()

    for slot in range(1, SLOTS):
        for copy in loads[slot]:
            copy.wait()
        build_integral(slot, xv, yv, order, xp, vs)

    build_swap(swap)
    turned = jnp.dot(drv[0], swap[...], preferred_element_type=F32)
    for j in range(NCHOL):
        driven[j] = turned[:, j * LANES : j * LANES + LANES]
    lane = lax.broadcasted_iota(jnp.int32, (1, LANES), 1)
    energy_a = jnp.zeros((1, LANES), F32)
    for a in range(TS):
        energy_a = jnp.where((lane & 31) == a, e_virt[TS * tiles[0, 0] + a], energy_a)
    row = lax.broadcasted_iota(jnp.int32, (ROWS, LANES), 0)
    energy_ij = jnp.zeros((ROWS, LANES), F32)
    for p in range(ROWS):
        energy_ij = jnp.where(row == p, e_occ[pairs[0, p]] + e_occ[pairs[1, p]], energy_ij)
    for j in range(NCHOL):
        energy_b = jnp.zeros((1, LANES), F32)
        for e in range(4):
            energy_b = jnp.where((lane >> 5) == e, e_virt[TS * tiles[0, 1] + 4 * j + e], energy_b)
        denominator[j] = (energy_a + energy_b) - energy_ij

    wish_copy(1 - core).wait_recv()
    share_picks(0)
    for slot in range(SLOTS):
        for j in range(NCHOL):
            w, h = j // 2, j % 2
            left[slot, w * ROWS : w * ROWS + ROWS, h * LANES : h * LANES + LANES] = arrived(0, j, slot)
    for step in range(1, NCHOL + 1):
        j = lax.rem(chol + step, NCHOL)
        if step < NCHOL:
            part[j] = ladder(j)
            sum_copy(chol, j).start()
        else:
            sums[chol] = ladder(j)

    def take_sum(step, carry):
        peer = lax.rem(chol + step, NCHOL)
        sum_copy(peer, peer).wait_recv()
        return carry

    lax.fori_loop(1, NCHOL, take_sum, 0)
    total = driven[chol]
    for j in range(NCHOL):
        total = total + sums[j]
    blocks[1, chip] = (-total / denominator[chol]).astype(BF16)
    gather_start(1)
    share_picks(1)
    for slot in range(SLOTS):
        for j in range(NCHOL):
            stack[slot * ROWS : slot * ROWS + ROWS, j * LANES : j * LANES + LANES] = arrived(1, j, slot)
    turned = jnp.dot(stack[...], swap[...], preferred_element_type=F32).astype(BF16)
    for slot in range(SLOTS):
        for w in range(4):
            left[slot, w * ROWS : w * ROWS + ROWS, :] = turned[
                slot * ROWS : slot * ROWS + ROWS, w * 256 : w * 256 + 256
            ]
    for half in range(2):
        for j in range(4):
            final[half, chol, j] = ladder(4 * half + j).astype(BF16)

        def send_final(step, carry, half=half):
            final_copy(half, chol, lax.rem(chol + step, NCHOL)).start()
            return carry

        lax.fori_loop(1, NCHOL, send_final, 0)
    for half in range(2):

        def take_final(step, carry, half=half):
            peer = lax.rem(chol + step, NCHOL)
            final_copy(half, peer, peer).wait_recv()
            return carry

        lax.fori_loop(1, NCHOL, take_final, 0)
        for j in range(4):
            total = driven[4 * half + j]
            for source in range(NCHOL):
                total = total + final[half, source, j].astype(F32)
            at = (4 * half + j) * LANES
            stack[0:ROWS, at : at + LANES] = (-total / denominator[4 * half + j]).astype(BF16)
    out[0] = jnp.dot(stack[0:ROWS, :], swap[...], preferred_element_type=F32).astype(BF16)

    wish_copy(core).wait_send()
    share_drain(0)
    share_drain(1)

    def drain_sums(step, carry):
        peer = lax.rem(chol + step, NCHOL)
        sum_copy(chol, peer).wait_send()
        for half in range(2):
            final_copy(half, chol, peer).wait_send()
        return carry

    lax.fori_loop(1, NCHOL, drain_sums, 0)


def shards(amplitudes, driver, x_tiles, y_tiles, sources, live, block_tiles, pairs, e_virt, e_occ):
    vmem = pl.BlockSpec(memory_space=pltpu.VMEM)
    hbm = pl.BlockSpec(memory_space=pl.ANY)
    dma = pltpu.SemaphoreType.DMA
    return pl.pallas_call(
        kernel,
        out_shape=jax.ShapeDtypeStruct((1, ROWS, TT), BF16),
        in_specs=[hbm] * 10,
        out_specs=vmem,
        scratch_shapes=[
            pltpu.SMEM((1, SLOTS), jnp.int32),
            pltpu.SMEM((1, SLOTS), jnp.int32),
            pltpu.SMEM((1, 2), jnp.int32),
            pltpu.SMEM((2, ROWS), jnp.int32),
            pltpu.SMEM((TT,), F32),
            pltpu.SMEM((LANES,), F32),
            pltpu.VMEM((1, ROWS, TT), BF16),
            pltpu.VMEM((1, ROWS, TT), BF16),
            pltpu.VMEM((SLOTS, DEPTH, TT), BF16),
            pltpu.VMEM((SLOTS, DEPTH, TT), BF16),
            pltpu.VMEM((TT, TT), BF16),
            pltpu.VMEM((TT, TT), BF16),
            pltpu.VMEM((DEPTH, TT), BF16),
            pltpu.VMEM((SLOTS, 256, 4096), BF16),
            pltpu.VMEM((SLOTS, 4 * ROWS, 256), BF16),
            pltpu.VMEM((SLOTS * ROWS, TT), BF16),
            pltpu.VMEM((2, 8, LANES), F32),
            pltpu.VMEM((2, NCHIP, ROWS, LANES), BF16),
            pltpu.VMEM((2, 2, SLOTS, ROWS, LANES), BF16),
            pltpu.VMEM((2, 2, NCHOL, SLOTS, ROWS, LANES), BF16),
            pltpu.VMEM((NCHOL, ROWS, LANES), F32),
            pltpu.VMEM((NCHOL, ROWS, LANES), F32),
            pltpu.VMEM((NCHOL, ROWS, LANES), F32),
            pltpu.VMEM((NCHOL, ROWS, LANES), F32),
            pltpu.VMEM((2, NCHOL, 4, ROWS, LANES), BF16),
            dma((8,)),
            dma((2 * SLOTS,)),
            dma,
            dma,
            dma((2, NCHIP)),
            dma((2, NCHIP)),
            dma((2, NPAIR)),
            dma((2, 2, NCHOL)),
            dma((NCHOL,)),
            dma((NCHOL,)),
            dma((2, NCHOL)),
            dma((2, NCHOL)),
        ],
        compiler_params=pltpu.CompilerParams(
            collective_id=0, has_side_effects=True, vmem_limit_bytes=67043328
        ),
        name="ladder_sweeps",
    )(sources, live, block_tiles, pairs.T, e_virt, e_occ, amplitudes, driver, x_tiles, y_tiles)


def solution(mesh):
    placed = (
        P("sec", None, None),
        P("sec", None, None),
        P("sec", None, "chol", None),
        P("sec", None, "chol", None),
        P("sec", None),
        P("sec", None),
        P("sec", None),
        P(),
        P(),
        P(),
    )
    return jax.shard_map(
        shards, mesh=mesh, in_specs=placed, out_specs=P("sec", None, None), check_vma=False
    )
```

time: 497 us -> 66.3 us (0.13); the launches traced: 491 us -> 66.2 us
  waiting for transfers between devices: 371 us -> 0 us
  Pallas kernels: 0 us -> 64.8 us
  local copies, waits for them, and re-layouts: 56.7 us -> 1.38 us
  matrix products: 38.3 us -> 0 us
  between operations: 22.7 us -> 0.01 us
    all_gather x2 -> x0, waiting for transfers between devices: 215 us -> none  [the longest x1 150 us: shards(): every = lax.all_gather(current, 'sec', axis=0, tiled=True)]
    psum x2 -> x0, waiting for transfers between devices: 155 us -> none  [shards(): summed = lax.psum(local_sum, 'chol')]
    pallas_call x0 -> x1, Pallas kernels: none -> 64.8 us  [shards(): pl.pallas_call(kernel, out_shape=jax.ShapeDtypeStruct((1, ROWS, TT), BF16...]
    dot_general x9 -> x0, matrix products: 38.3 us -> none  [the longest x3 23.7 us: integral(): lax.dot_general(left_tile, right_tile, (((0,), (0,)), ((), ())), preferre...]
    convert_element_type x3 -> x0, local copies, waits for them, and re-layouts: 36.2 us -> none  [integral(): return product.reshape(TS * TS, TS * TS).astype(jnp.bfloat16)]
    dot_general x8 -> x0, local copies, waits for them, and re-layouts: 15.3 us -> none  [integral(): lax.dot_general(left_tile, right_tile, (((0,), (0,)), ((), ())), preferre...]
  transfers between devices with their start and end apart: 4 -> 0, of which waited for: 4 -> 0; matrix products, arithmetic and copies ran while one was open for 16% -> 0% of each run, Pallas kernels for 0% -> 0%
where the time goes in v2:
time: 66.3 us; the launch traced here: 66.2 us
  Pallas kernels  64.8 us (98%)
  local copies, waits for them, and re-layouts  1.38 us (2%)
    pallas_call x1, Pallas kernels, shards(): pl.pallas_call(kernel, out_shape=jax.ShapeDtypeStruct((1, ROWS, TT), BF16...  64.8 us
    unnamed x1, local copies, waits for them, and re-layouts  1.38 us

profile of v2, /device:TPU:1, one launch (start us, length us, event | category | flops | bytes accessed | tf_op | source)
XLA Modules:
  0.0 66.2 jit_solution(15663457421449067946)
XLA Ops:
  0.0 64.8 %ladder_sweeps.1 = bf16[1,16,1024]{2,1,0:T(8,128)(2,1)} custom-call(s32[1,3]{1,0:T(1,128)} %sources_hbm.1, s32[1,3]{1,0:T(1,128)} %live_hbm.1, s32[1,2]{1,0:T(1,128)} %tiles_hbm.1, s32[2,16]{1,0:T(2,128)} %bitcast.1, f32[1024]{0:T(1024)} %e_virt_hbm.1, f32[128]{0:T(128)} %e_occ_hbm.1, bf16[1,16,1024]{2,1,0:T(8,128)(2,1)} %amp_hbm.1, ...), custom_call_target="tpu_custom_call" | custom-call | tf_op jit(solution)/shard_map/ladder_sweeps/pallas_call | solution.py:377
  64.8 1.4 %copy.12 = bf16[1,16,1024]{2,1,0:T(8,128)(2,1)} copy(bf16[1,16,1024]{2,1,0:T(8,128)(2,1)} %ladder_sweeps.1) | data formatting | bytes 65536

commit v3 on v2

--- a/solution.py
+++ b/solution.py
@@ -166,11 +166,6 @@
         )
 
     def share_picks(turn):
-        def take_block(step, carry):
-            gather_copy(turn, far_chip(step), step).wait_recv()
-            return carry
-
-        lax.fori_loop(0, NCHIP - 1, take_block, 0)
         asked = [
             jnp.broadcast_to(wishes[half, slot : slot + 1, :], (ROWS, LANES))
             for half in range(2)
@@ -182,7 +177,14 @@
             name = (2 * source + core).astype(F32)
             return tuple(jnp.where(a == name, block, f) for a, f in zip(asked, found))
 
-        found = lax.fori_loop(0, NCHIP, look, (jnp.zeros((ROWS, LANES), F32),) * (2 * SLOTS))
+        def take_block(step, found):
+            back = NCHIP - 2 - step
+            source = far_chip(back)
+            gather_copy(turn, source, back).wait_recv()
+            return look(source, found)
+
+        found = look(chip, (jnp.zeros((ROWS, LANES), F32),) * (2 * SLOTS))
+        found = lax.fori_loop(0, NCHIP - 1, take_block, found)
         for half in range(2):
             for slot in range(SLOTS):
                 offers[turn, half, slot] = found[SLOTS * half + slot].astype(BF16)
@@ -321,6 +323,8 @@
         total = total + sums[j]
     blocks[1, chip] = (-total / denominator[chol]).astype(BF16)
     gather_start(1)
+    wish_copy(core).wait_send()
+    share_drain(0)
     share_picks(1)
     for slot in range(SLOTS):
         for j in range(NCHOL):
@@ -340,6 +344,13 @@
             return carry
 
         lax.fori_loop(1, NCHOL, send_final, 0)
+    share_drain(1)
+
+    def drain_sums(step, carry):
+        sum_copy(chol, lax.rem(chol + step, NCHOL)).wait_send()
+        return carry
+
+    lax.fori_loop(1, NCHOL, drain_sums, 0)
     for half in range(2):
 
         def take_final(step, carry, half=half):
@@ -356,24 +367,21 @@
             stack[0:ROWS, at : at + LANES] = (-total / denominator[4 * half + j]).astype(BF16)
     out[0] = jnp.dot(stack[0:ROWS, :], swap[...], preferred_element_type=F32).astype(BF16)
 
-    wish_copy(core).wait_send()
-    share_drain(0)
-    share_drain(1)
-
-    def drain_sums(step, carry):
-        peer = lax.rem(chol + step, NCHOL)
-        sum_copy(chol, peer).wait_send()
+    def drain_final(step, carry):
         for half in range(2):
-            final_copy(half, chol, peer).wait_send()
-        return carry
-
-    lax.fori_loop(1, NCHOL, drain_sums, 0)
+            final_copy(half, chol, lax.rem(chol + step, NCHOL)).wait_send()
+        return carry
+
+    lax.fori_loop(1, NCHOL, drain_final, 0)
 
 
 def shards(amplitudes, driver, x_tiles, y_tiles, sources, live, block_tiles, pairs, e_virt, e_occ):
     vmem = pl.BlockSpec(memory_space=pltpu.VMEM)
-    hbm = pl.BlockSpec(memory_space=pl.ANY)
+    hbm = pl.BlockSpec(memory_space=pltpu.HBM)
     dma = pltpu.SemaphoreType.DMA
+    operands = (
+        sources, live, block_tiles, pairs.T, e_virt, e_occ, amplitudes, driver, x_tiles, y_tiles,
+    )
     return pl.pallas_call(
         kernel,
         out_shape=jax.ShapeDtypeStruct((1, ROWS, TT), BF16),
@@ -419,10 +427,10 @@
             dma((2, NCHOL)),
         ],
         compiler_params=pltpu.CompilerParams(
-            collective_id=0, has_side_effects=True, vmem_limit_bytes=67043328
+            collective_id=0, has_side_effects=True, vmem_limit_bytes=48 * 1024 * 1024
         ),
         name="ladder_sweeps",
-    )(sources, live, block_tiles, pairs.T, e_virt, e_occ, amplitudes, driver, x_tiles, y_tiles)
+    )(*(pltpu.with_memory_space_constraint(operand, pltpu.HBM) for operand in operands))
 
 
 def solution(mesh):

time: 66.3 us -> 63.1 us (0.952)
  Pallas kernels: 64.8 us -> 62.4 us
  local copies, waits for them, and re-layouts: 1.38 us -> 0.62 us
    pallas_call x1, Pallas kernels: 64.8 us -> 62.4 us  [shards(): pl.pallas_call(kernel, out_shape=jax.ShapeDtypeStruct((1, ROWS, TT), BF16...]
    unnamed x1, local copies, waits for them, and re-layouts: 1.38 us -> 0.62 us
where the time goes in v3:
time: 63.1 us; the launch traced here: 63 us
  Pallas kernels  62.4 us (99%)
    pallas_call x1, Pallas kernels, shards(): pl.pallas_call(kernel, out_shape=jax.ShapeDtypeStruct((1, ROWS, TT), BF16...  62.4 us

profile of v3, /device:TPU:1, one launch (start us, length us, event | category | flops | bytes accessed | tf_op | source)
XLA Modules:
  0.0 63.0 jit_solution(165979977764628194)
XLA Ops:
  0.0 62.4 %ladder_sweeps.1 = bf16[1,16,1024]{2,1,0:T(8,128)(2,1)S(1)} custom-call(s32[1,3]{1,0:T(1,128)} %sources_hbm.1, s32[1,3]{1,0:T(1,128)} %live_hbm.1, s32[1,2]{1,0:T(1,128)} %tiles_hbm.1, s32[2,16]{1,0:T(2,128)} %bitcast.1, f32[1024]{0:T(1024)} %e_virt_hbm.1, f32[128]{0:T(128)} %e_occ_hbm.1, bf16[1,16,1024]{2,1,0:T(8,128)(2,1)} %amp_hbm.1, ...), custom_call_target="tpu_custom_call" | custom-call | tf_op jit(solution)/shard_map/ladder_sweeps/pallas_call | solution.py:385
  62.4 0.6 copy.12

commit v4 on v3

--- a/solution.py
+++ b/solution.py
@@ -17,6 +17,10 @@
 MESH = pl.DeviceIdType.MESH
 F32 = jnp.float32
 BF16 = jnp.bfloat16
+
+
+def rem(value, size):
+    return value % size if isinstance(value, int) else lax.rem(value, size)
 
 
 def build_column_order(order):
@@ -72,12 +76,12 @@
 
     def far_chip(step):
         turn = step // 2
-        away = 8 + (1 - 2 * lax.rem(turn, 2)) * ((turn + 1) // 2)
-        side = 1 - lax.rem(step, 2)
+        away = 8 + (1 - 2 * rem(turn, 2)) * ((turn + 1) // 2)
+        side = 1 - rem(step, 2)
         return lax.rem(x_hi + side, 2) * 16 + lax.rem(z + away, 16)
 
     def near_core(step):
-        return lax.rem(core + lax.rem(step, 2), 2)
+        return lax.rem(core + rem(step, 2), 2)
 
     def near_chol(step):
         return lax.rem(chol + step // 2, NCHOL)
@@ -93,13 +97,15 @@
         )
         return carry
 
-    lax.fori_loop(0, NCHIP - 1, greet, 0)
+    for step in range(NCHIP - 1):
+        greet(step, 0)
 
     def greet_near(step, carry):
         pl.semaphore_signal(barrier, inc=1, device_id=near(step), device_id_type=MESH)
         return carry
 
-    lax.fori_loop(1, NPAIR, greet_near, 0)
+    for step in range(1, NPAIR):
+        greet_near(step, 0)
 
     small = [
         pltpu.make_async_copy(source, target, small_sem.at[place])
@@ -149,11 +155,8 @@
         )
 
     def gather_start(turn):
-        def send(step, carry):
+        for step in range(NCHIP - 1):
             gather_copy(turn, chip, step).start()
-            return carry
-
-        lax.fori_loop(0, NCHIP - 1, send, 0)
 
     def pick_copy(turn, half, column, step):
         return pltpu.make_async_remote_copy(
@@ -189,11 +192,8 @@
             for slot in range(SLOTS):
                 offers[turn, half, slot] = found[SLOTS * half + slot].astype(BF16)
 
-        def send(step, carry):
+        for step in range(1, NPAIR):
             pick_copy(turn, core, chol, step).start()
-            return carry
-
-        lax.fori_loop(1, NPAIR, send, 0)
         picked[turn, core, chol] = offers[turn, core]
 
         def take(step, carry):

time: 63.1 us -> 62.9 us (level)
  no operation moved by 1% of the time
where the time goes in v4:
time: 62.9 us; the launch traced here: 62.8 us
  Pallas kernels  62.2 us (99%)
    pallas_call x1, Pallas kernels, shards(): pl.pallas_call(kernel, out_shape=jax.ShapeDtypeStruct((1, ROWS, TT), BF16...  62.2 us

profile of v4, /device:TPU:1, one launch (start us, length us, event | category | flops | bytes accessed | tf_op | source)
XLA Modules:
  0.0 62.8 jit_solution(12497514849266693858)
XLA Ops:
  0.0 62.2 %ladder_sweeps.1 = bf16[1,16,1024]{2,1,0:T(8,128)(2,1)S(1)} custom-call(s32[1,3]{1,0:T(1,128)} %sources_hbm.1, s32[1,3]{1,0:T(1,128)} %live_hbm.1, s32[1,2]{1,0:T(1,128)} %tiles_hbm.1, s32[2,16]{1,0:T(2,128)} %bitcast.1, f32[1024]{0:T(1024)} %e_virt_hbm.1, f32[128]{0:T(128)} %e_occ_hbm.1, bf16[1,16,1024]{2,1,0:T(8,128)(2,1)} %amp_hbm.1, ...), custom_call_target="tpu_custom_call" | custom-call | tf_op jit(solution)/shard_map/ladder_sweeps/pallas_call | solution.py:385
  62.2 0.6 copy.12
